TPU v7x, 32 devices: a whole 2x2x4 slice. The times are simulated.
32 devices in a mesh: conv: 4 (over y, core), seq: 4 (over z), tensor: 2 (over x).
Axes of the slice: x: 2, y: 2, z: 4, core: 2. Of those that a mesh axis runs over, the one named last changes fastest.
Arguments:
- queries: bfloat16 [4, 512, 4096], P('conv', 'seq', 'tensor'), may hold values from -6 to 6
- keys: bfloat16 [8, 1664, 1024], P('conv', ('seq', 'tensor')), may hold values from -6 to 6
- values: bfloat16 [8, 1664, 1024], P('conv', ('seq', 'tensor')), may hold values from -18 to 18
- q_gain: float32 [128], replicated, may hold values from 0.9 to 2.2
- k_gain: float32 [128], replicated, may hold values from 0.9 to 2.2
- gate: float32 [1], replicated, may hold values from 0.4 to 1.6
- tile_count: int32 [4], replicated, may hold values from 1 to 2, as said below
- tile_owner: int32 [4, 2], replicated, may hold values from -1 to 3, as said below
- visible: int32 [4, 512], replicated, may hold values from 0 to 2, as said below
- d_out: bfloat16 [4, 512, 4096], P('conv', 'seq', 'tensor'), may hold values from -12 to 12
Outputs:
- attended: bfloat16 [4, 512, 4096], P('conv', 'seq', 'tensor')
- d_queries: bfloat16 [4, 512, 4096], P('conv', 'seq', 'tensor')
- d_keys: bfloat16 [8, 1664, 1024], P('conv', ('seq', 'tensor'))
- d_values: bfloat16 [8, 1664, 1024], P('conv', ('seq', 'tensor'))
Inputs may be any that keep to these rules, and one draw needn't show every extreme that they name: `tile_count`: some conversation has 2 tiles. `tile_owner`: entries with t at or past the conversation's count are -1. The tiles of one conversation have different owners, no two tiles share a slot, and some conv index holds 2 tiles. `visible`: never falls along a conversation's text; it is 0 at the first token and 2 at the last.
All inputs are finite; a program needn't handle non-finite values.
Results may differ from a plain program's by a relative error of at most 0.02.
Values may be sent and summed in bfloat16 or wider, within the bound.
A program may use at most 128 MiB of HBM per device.

v0:
```python
from functools import partial
import math
import jax
import jax.numpy as jnp
from jax import lax
from jax.sharding import PartitionSpec as P

TILE = 1601
EPSILON = 1e-05


def head_norm(inputs, norm_gain):
    mean_square = jnp.mean(inputs * inputs, axis=-1, keepdims=True)
    return inputs * lax.rsqrt(mean_square + EPSILON) * norm_gain


def key_mask(seen_tiles, tile_index, row_start, row_count):
    row_ids = row_start + jnp.arange(row_count, dtype=jnp.int32)
    return (seen_tiles > tile_index)[:, None] & (row_ids < TILE)[None, :]


def tile_weights(query_bf, key_tile, visible_keys, score_scale):
    scores = (
        jnp.einsum("pkgd,rkd->kgpr", query_bf, key_tile, preferred_element_type=jnp.float32)
        * score_scale
    )
    return jnp.where(visible_keys[None, None], jnp.exp(scores), 0.0)


def tile_forward(query_bf, key_tile, value_tile, visible_keys, score_scale):
    weights = tile_weights(query_bf, key_tile, visible_keys, score_scale)
    weighted = jnp.einsum(
        "kgpr,rkd->pkgd",
        weights.astype(jnp.bfloat16),
        value_tile,
        preferred_element_type=jnp.float32,
    )
    return (jnp.sum(weights, axis=-1), weighted)


def tile_gradients(
    query_bf,
    grad_bf,
    key_tile,
    value_tile,
    visible_keys,
    safe_sum,
    row_delta,
    score_scale,
    block_count,
):
    weights = tile_weights(query_bf, key_tile, visible_keys, score_scale)
    probability = weights / safe_sum[..., None]
    grad_prob = jnp.einsum(
        "pkgd,rkd->kgpr", grad_bf, value_tile, preferred_element_type=jnp.float32
    )
    grad_score = (probability * (grad_prob - row_delta[..., None])).astype(jnp.bfloat16)
    prob_bf = probability.astype(jnp.bfloat16)
    grad_query = (
        jnp.einsum("kgpr,rkd->pkgd", grad_score, key_tile, preferred_element_type=jnp.float32)
        * score_scale
    )
    kv_local, group_size, token_count, row_count = grad_score.shape
    head_size = query_bf.shape[-1]
    block_tokens = token_count // block_count
    score_blocks = grad_score.reshape(kv_local, group_size, block_count, block_tokens, row_count)
    prob_blocks = prob_bf.reshape(kv_local, group_size, block_count, block_tokens, row_count)
    query_blocks = query_bf.reshape(block_count, block_tokens, kv_local, group_size, head_size)
    grad_blocks = grad_bf.reshape(block_count, block_tokens, kv_local, group_size, head_size)
    key_part = (
        jnp.einsum(
            "kgbpr,bpkgd->brkd", score_blocks, query_blocks, preferred_element_type=jnp.float32
        )
        * score_scale
    )
    value_part = jnp.einsum(
        "kgbpr,bpkgd->brkd", prob_blocks, grad_blocks, preferred_element_type=jnp.float32
    )
    key_part = jnp.sum(
        lax.optimization_barrier(key_part.astype(jnp.bfloat16)).astype(jnp.float32), axis=0
    )
    value_part = jnp.sum(
        lax.optimization_barrier(value_part.astype(jnp.bfloat16)).astype(jnp.float32), axis=0
    )
    return (
        grad_query,
        key_part.reshape(row_count, kv_local * head_size),
        value_part.reshape(row_count, kv_local * head_size),
    )


def attend_forward(query_bf, tile_keys, tile_values, seen_tiles, row_start, score_scale):
    row_count, slot_count, features = tile_keys.shape
    token_count, kv_local, group_size, head_size = query_bf.shape
    weight_sum = jnp.zeros((kv_local, group_size, token_count), jnp.float32)
    weighted = jnp.zeros(query_bf.shape, jnp.float32)
    for tile_index in range(slot_count):
        key_tile = tile_keys[:, tile_index].reshape(row_count, kv_local, head_size)
        value_tile = tile_values[:, tile_index].reshape(row_count, kv_local, head_size)
        visible_keys = key_mask(seen_tiles, tile_index, row_start, row_count)
        work = partial(tile_forward, query_bf, key_tile, value_tile, visible_keys, score_scale)
        part_sum, part_weighted = work()
        weight_sum = weight_sum + part_sum
        weighted = weighted + part_weighted
    return (weight_sum, weighted)


def attend_backward(
    query_bf,
    grad_bf,
    tile_keys,
    tile_values,
    seen_tiles,
    row_start,
    safe_sum,
    row_delta,
    score_scale,
    block_tokens,
):
    row_count, slot_count, features = tile_keys.shape
    token_count, kv_local, group_size, head_size = query_bf.shape
    block_count = token_count // block_tokens
    grad_query = jnp.zeros(query_bf.shape, jnp.float32)
    key_parts = []
    value_parts = []
    for tile_index in range(slot_count):
        key_tile = tile_keys[:, tile_index].reshape(row_count, kv_local, head_size)
        value_tile = tile_values[:, tile_index].reshape(row_count, kv_local, head_size)
        visible_keys = key_mask(seen_tiles, tile_index, row_start, row_count)
        work = partial(
            tile_gradients,
            query_bf,
            grad_bf,
            key_tile,
            value_tile,
            visible_keys,
            safe_sum,
            row_delta,
            score_scale,
            block_count,
        )
        part_query, key_part, value_part = work()
        grad_query = grad_query + part_query
        key_parts.append(key_part)
        value_parts.append(value_part)
    return (grad_query, jnp.stack(key_parts, axis=1), jnp.stack(value_parts, axis=1))


def shards(queries, keys, values, q_gain, k_gain, gate, tile_count, tile_owner, visible, d_out):
    conv_count = lax.axis_size("conv")
    tensor_count = lax.axis_size("tensor")
    conv_index = lax.axis_index("conv")
    sequence_index = lax.axis_index("seq")
    slot_count, row_local, features = keys.shape
    head_size = q_gain.shape[0]
    kv_heads = features // head_size
    kv_local = kv_heads // tensor_count
    token_count = queries.shape[1]
    query_heads = queries.shape[2] // head_size
    group_size = query_heads // kv_local
    score_scale = 1.0 / math.sqrt(head_size)
    gate_value = jnp.tanh(gate[0])
    conv_ids = jnp.arange(conv_count, dtype=jnp.int32)
    transfers = (tile_owner == conv_index).astype(jnp.bfloat16)
    own_owners = lax.dynamic_index_in_dim(tile_owner, conv_index, 0, keepdims=False)
    takes = (own_owners[:, None] == conv_ids[None, :]).astype(jnp.bfloat16)
    own_count = lax.dynamic_index_in_dim(tile_count, conv_index, 0, keepdims=False)
    seen_all = jnp.minimum(
        lax.dynamic_index_in_dim(visible, conv_index, 0, keepdims=False), own_count
    )
    key_raw = keys.astype(jnp.float32).reshape(slot_count, row_local, kv_heads, head_size)
    key_normed, key_back = jax.vjp(lambda inputs: head_norm(inputs, k_gain), key_raw)
    key_halfprec = key_normed.astype(jnp.bfloat16).reshape(slot_count, row_local, features)
    outgoing_keys = jnp.einsum(
        "wn,nki->wki", transfers, key_halfprec, preferred_element_type=jnp.float32
    ).astype(jnp.bfloat16)
    send_values = jnp.einsum(
        "wn,nki->wki", transfers, values, preferred_element_type=jnp.float32
    ).astype(jnp.bfloat16)
    got_keys, got_values = (
        lax.all_to_all(
            lax.all_to_all(outgoing_keys, "conv", split_axis=0, concat_axis=0, tiled=True),
            "tensor",
            split_axis=2,
            concat_axis=1,
            tiled=True,
        ),
        lax.all_to_all(
            lax.all_to_all(send_values, "conv", split_axis=0, concat_axis=0, tiled=True),
            "tensor",
            split_axis=2,
            concat_axis=1,
            tiled=True,
        ),
    )
    tile_keys = jnp.einsum(
        "to,orf->rtf", takes, got_keys, preferred_element_type=jnp.float32
    ).astype(jnp.bfloat16)
    tile_values = jnp.einsum(
        "to,orf->rtf", takes, got_values, preferred_element_type=jnp.float32
    ).astype(jnp.bfloat16)
    query_raw = queries[0].astype(jnp.float32).reshape(token_count, query_heads, head_size)
    query_normed, query_back = jax.vjp(lambda inputs: head_norm(inputs, q_gain), query_raw)
    query_bf = query_normed.astype(jnp.bfloat16).reshape(
        token_count, kv_local, group_size, head_size
    )
    grad_bf = (
        (gate_value * d_out[0].astype(jnp.float32))
        .astype(jnp.bfloat16)
        .reshape(token_count, kv_local, group_size, head_size)
    )
    own_start = sequence_index * token_count
    all_queries = lax.all_gather(query_bf, "seq", axis=0, tiled=True)
    all_grads = lax.all_gather(grad_bf, "seq", axis=0, tiled=True)
    share_rows = tile_keys.shape[0]
    row_start = sequence_index * share_rows
    part_sum, part_weighted = attend_forward(
        all_queries, tile_keys, tile_values, seen_all, row_start, score_scale
    )
    all_weighted, all_weight_sum = (
        lax.psum(part_weighted.astype(jnp.bfloat16), "seq").astype(jnp.float32),
        lax.psum(part_sum.astype(jnp.bfloat16), "seq").astype(jnp.float32),
    )
    safe_all = jnp.where(all_weight_sum > 0, all_weight_sum, 1.0)
    context_all = all_weighted / jnp.transpose(safe_all, (2, 0, 1))[..., None]
    context = lax.dynamic_slice_in_dim(context_all, own_start, token_count, 0)
    row_delta = jnp.transpose(
        jnp.sum(all_grads.astype(jnp.float32) * context_all, axis=-1), (1, 2, 0)
    )
    grad_part, key_sums, value_sums = attend_backward(
        all_queries,
        all_grads,
        tile_keys,
        tile_values,
        seen_all,
        row_start,
        safe_all,
        row_delta,
        score_scale,
        token_count,
    )
    grad_query = lax.psum_scatter(
        grad_part.astype(jnp.bfloat16), "seq", scatter_dimension=0, tiled=True
    ).astype(jnp.float32)
    attended = (
        (gate_value * context).astype(jnp.bfloat16).reshape(1, token_count, query_heads * head_size)
    )
    key_round = key_sums.astype(jnp.bfloat16)
    value_round = value_sums.astype(jnp.bfloat16)
    back_keys = jnp.einsum(
        "to,rtf->orf", takes, key_round, preferred_element_type=jnp.float32
    ).astype(jnp.bfloat16)
    back_values = jnp.einsum(
        "to,rtf->orf", takes, value_round, preferred_element_type=jnp.float32
    ).astype(jnp.bfloat16)
    returned_keys, returned_values = (
        lax.all_to_all(
            lax.all_to_all(back_keys, "conv", split_axis=0, concat_axis=0, tiled=True),
            "tensor",
            split_axis=1,
            concat_axis=2,
            tiled=True,
        ),
        lax.all_to_all(
            lax.all_to_all(back_values, "conv", split_axis=0, concat_axis=0, tiled=True),
            "tensor",
            split_axis=1,
            concat_axis=2,
            tiled=True,
        ),
    )
    positioned_keys = jnp.einsum(
        "ew,eig->wig", transfers, returned_keys, preferred_element_type=jnp.float32
    )
    d_values = jnp.einsum(
        "ew,eig->wig", transfers, returned_values, preferred_element_type=jnp.float32
    ).astype(jnp.bfloat16)
    d_keys = key_back(positioned_keys.reshape(slot_count, row_local, kv_heads, head_size))[0]
    d_keys = d_keys.astype(jnp.bfloat16).reshape(slot_count, row_local, features)
    d_queries = query_back(grad_query.reshape(token_count, query_heads, head_size))[0]
    d_queries = d_queries.astype(jnp.bfloat16).reshape(1, token_count, query_heads * head_size)
    return (attended, d_queries, d_keys, d_values)


def solution(mesh):
    in_specs = (
        P("conv", "seq", "tensor"),
        P("conv", ("seq", "tensor"), None),
        P("conv", ("seq", "tensor"), None),
        P(),
        P(),
        P(),
        P(),
        P(),
        P(),
        P("conv", "seq", "tensor"),
    )
    out_specs = (
        P("conv", "seq", "tensor"),
        P("conv", "seq", "tensor"),
        P("conv", ("seq", "tensor"), None),
        P("conv", ("seq", "tensor"), None),
    )
    return jax.shard_map(shards, mesh=mesh, in_specs=in_specs, out_specs=out_specs, check_vma=False)
```

profile of v0, /device:TPU:0, one launch (start us, length us, event | category | flops | bytes accessed | tf_op | source)
XLA Modules:
  0.0 426.6 jit_solution(4525607871681992089)
XLA Ops:
  29.1 16.1 %all-to-all-done.2 = bf16[4,208,1024]{2,1,0:T(8,128)(2,1)} async-done(((bf16[4,208,1024]{2,1,0:T(8,128)(2,1)}), bf16[4,208,1024]{2,1,0:T(8,128)(2,1)}, u32[]{:S(2)}, u32[]{:S(2)}) %all-to-all-start.2) | async-done | bytes 1703968 | tf_op jit(solution)/shard_map/all_to_all | solution.py:182
  53.0 17.2 %all-to-all-done = bf16[4,208,1024]{2,1,0:T(8,128)(2,1)S(1)} async-done(((bf16[4,208,1024]{2,1,0:T(8,128)(2,1)}), bf16[4,208,1024]{2,1,0:T(8,128)(2,1)S(1)}, u32[]{:S(2)}, u32[]{:S(2)}) %all-to-all-start) | async-done | bytes 1703968 | tf_op jit(solution)/shard_map/all_to_all | solution.py:189
  83.4 17.2 %all-to-all-done.3 = bf16[4,208,1024]{1,0,2:T(4,128)(2,1)S(1)} async-done(((bf16[4,208,1024]{1,0,2:T(4,128)(2,1)}), bf16[4,208,1024]{1,0,2:T(4,128)(2,1)S(1)}, u32[]{:S(2)}, u32[]{:S(2)}) %all-to-all-start.3) | async-done | bytes 1703968 | tf_op jit(solution)/shard_map/all_to_all | solution.py:181
  100.6 4.8 %all-to-all-start.1 = ((bf16[4,208,1024]{1,0,2:T(4,128)(2,1)}), bf16[4,208,1024]{1,0,2:T(4,128)(2,1)}, u32[]{:S(2)}, u32[]{:S(2)}) async-start(bf16[4,208,1024]{1,0,2:T(4,128)(2,1)} %copy.190), calls=%async_computation.1 | async-start | bytes 4194304 | tf_op jit(solution)/shard_map/all_to_all | solution.py:188
  117.9 12.1 %all-to-all-done.1 = bf16[4,208,1024]{1,0,2:T(4,128)(2,1)} async-done(((bf16[4,208,1024]{1,0,2:T(4,128)(2,1)}), bf16[4,208,1024]{1,0,2:T(4,128)(2,1)}, u32[]{:S(2)}, u32[]{:S(2)}) %all-to-all-start.1) | async-done | bytes 1703968 | tf_op jit(solution)/shard_map/all_to_all | solution.py:188
  129.9 5.4 %copy.191 = bf16[4,208,2,512]{3,0,1,2:T(4,128)(2,1)S(1)} copy(bf16[4,208,2,512]{1,0,3,2:T(4,128)(2,1)} %bitcast.2) | data formatting | bytes 3407872 | tf_op jit(solution)/shard_map/all_to_all | solution.py:188
  140.4 8.4 %fusion.8 = (f32[4,4,512]{2,1,0:T(4,128)S(1)}, f32[4,416,512,4]{2,1,3,0:T(8,128)}) fusion(pred[512,416]{0,1:T(8,128)(4,1)S(1)} %get-tuple-element.37, bf16[512,4,4,128]{3,0,2,1:T(8,128)(2,1)} %all-gather.3.cloned.1.call-done, bf16[416,4,128,1]{2,1,0,3:T(4,128)(2,1)S(1)} %bitcast.268), kind=kOutput, calls=%fused_computation.12 | convolution fusion | flops 882630656 | bytes 16400384 | tf_op jit(solution)/shard_map/pkgd,rkd->kgpr/dot_general | solution.py:24
  148.8 6.6 %fusion.5 = (f32[4,4,512]{2,1,0:T(4,128)S(1)}, f32[4,416,512,4]{2,1,3,0:T(8,128)}) fusion(pred[512,416]{0,1:T(8,128)(4,1)S(1)} %get-tuple-element.36, bf16[512,4,4,128]{3,0,2,1:T(8,128)(2,1)S(1)} %copy-done.38, bf16[416,4,128,1]{2,1,0,3:T(4,128)(2,1)S(1)} %bitcast.270), kind=kOutput, calls=%fused_computation.9 | convolution fusion | flops 882630656 | bytes 16400384 | tf_op jit(solution)/shard_map/pkgd,rkd->kgpr/dot_general | solution.py:24
  155.5 19.6 %psum.15 = bf16[4,4,512]{2,1,0:T(4,128)(2,1)S(1)} all-reduce(bf16[4,4,512]{2,1,0:T(4,128)(2,1)S(1)} %add_convert_fusion.1), channel_id=1, replica_groups=mesh['conv'=4,'seq'=4,'tensor'=2] {'seq'}, use_global_device_ids=true, to_apply=%region_5.6 | all-reduce | flops 8192 | bytes 32768 | tf_op jit(solution)/shard_map/psum | solution.py:222
  175.0 6.4 %fusion.10 = f32[4,128,4,512]{3,1,2,0:T(8,128)S(1)} fusion(f32[4,416,512,4]{2,1,3,0:T(8,128)} %get-tuple-element.41, pred[512,416]{0,1:T(8,128)(4,1)S(1)} %get-tuple-element.37, bf16[416,4,128,1]{2,1,0,3:T(4,128)(2,1)S(1)} %bitcast.262), kind=kOutput, calls=%fused_computation.14 | convolution fusion | flops 882638848 | bytes 18464768 | tf_op jit(solution)/shard_map/kgpr,rkd->pkgd/dot_general | solution.py:32
  187.7 15.6 %convert_bitcast_fusion.1 = (bf16[4,4,52,4,8,128]{5,4,3,2,1,0:T(8,128)(2,1)}, bf16[4,4,52,4,8,128]{5,4,3,2,1,0:T(8,128)(2,1)}) fusion(f32[4,4,512]{2,1,0:T(4,128)S(1)} %get-tuple-element.34, f32[4,416,512,4]{2,1,3,0:T(8,128)} %get-tuple-element.39, pred[512,416]{0,1:T(8,128)(4,1)S(1)} %get-tuple-element.36, f32[4,416,512,4]{2,1,3,0:T(8,128)} %get-tuple-element.41, ...), kind=kLoop, calls=%fused_computation.29 | loop fusion | flops 27262976 | bytes 41353216
  208.5 6.7 %fusion.62 = bf16[4,416,4,128]{3,1,2,0:T(8,128)(2,1)} fusion(bf16[4,128,4,4,128]{4,1,3,2,0:T(8,128)(2,1)} %copy.227, bf16[4,4,52,4,8,128]{5,4,3,2,1,0:T(8,128)(2,1)} %get-tuple-element.32), kind=kOutput, calls=%fused_computation.69 | convolution fusion | flops 873267200 | bytes 10616832 | tf_op jit(solution)/shard_map/kgbpr,bpkgd->brkd/dot_general | solution.py:76
  223.5 6.1 %fusion.65 = bf16[4,416,4,128]{3,1,2,0:T(8,128)(2,1)} fusion(bf16[4,128,4,4,128]{4,1,3,2,0:T(8,128)(2,1)S(1)} %copy-done.17, bf16[4,4,52,4,8,128]{5,4,3,2,1,0:T(8,128)(2,1)} %get-tuple-element.33), kind=kOutput, calls=%fused_computation.70 | convolution fusion | flops 873267200 | bytes 10616832 | tf_op jit(solution)/shard_map/kgbpr,bpkgd->brkd/dot_general | solution.py:76
  238.0 4.4 %all-to-all-start.6 = ((bf16[4,416,512]{2,1,0:T(8,128)(2,1)}), bf16[4,416,512]{2,1,0:T(8,128)(2,1)}, u32[]{:S(2)}, u32[]{:S(2)}) async-start(bf16[4,416,512]{2,1,0:T(8,128)(2,1)} %copy.235), calls=%async_computation.6 | async-start | bytes 3407872 | tf_op jit(solution)/shard_map/all_to_all | solution.py:265
  242.5 28.4 %all-reduce.2.cloned.1.call-done = bf16[512,4,4,128]{0,3,2,1:T(8,128)(2,1)} async-done(((bf16[512,4,4,128]{0,3,2,1:T(8,128)(2,1)}), bf16[512,4,4,128]{0,3,2,1:T(8,128)(2,1)}) %all-reduce.2.cloned.1.call-update) | async-done | bytes 2097168 | tf_op jit(solution)/shard_map/psum | solution.py:221
  270.9 4.5 %multiply_reduce_fusion = (f32[512,4,4]{0,2,1:T(4,128)S(1)}, f32[512,4,4,128]{0,3,2,1:T(8,128)}) fusion(bf16[512,4,4,128]{0,3,2,1:T(8,128)(2,1)S(1)} %copy-done.8, f32[512,4,4]{0,2,1:T(4,128)S(1)} %get-tuple-element.35, bf16[512,4,4,128]{0,3,2,1:T(8,128)(2,1)} %all-reduce.2.cloned.1.call-done), kind=kLoop, calls=%fused_computation.37 | loop fusion | flops 5234688 | bytes 8454144 | tf_op jit(solution)/shard_map/reduce_sum | solution.py:228
  275.4 7.5 %fusion.1 = bf16[4,4,512,416]{2,3,1,0:T(8,128)(2,1)S(1)} fusion(bf16[512,4,4,128]{0,3,2,1:T(8,128)(2,1)S(1)} %copy-done.8, f32[4,4,512]{2,1,0:T(4,128)S(1)} %bitcast.273, f32[4,4,512]{2,1,0:T(4,128)S(1)} %get-tuple-element.34, f32[4,416,512,4]{2,1,3,0:T(8,128)} %get-tuple-element.41, pred[512,416]{0,1:T(8,128)(4,1)S(1)} %get-tuple-element.37, ...), kind=kOutput, calls=%fused_computation.2 | convolution fusion | flops 892862464 | bytes 23248896 | tf_op jit(solution)/shard_map/pkgd,rkd->kgpr/dot_general | solution.py:54
  293.5 7.3 %fusion.3 = bf16[4,4,512,416]{2,3,1,0:T(8,128)(2,1)S(1)} fusion(bf16[512,4,4,128]{0,3,2,1:T(8,128)(2,1)S(1)} %copy-done.8, f32[4,4,512]{2,1,0:T(4,128)S(1)} %bitcast.274, f32[4,4,512]{2,1,0:T(4,128)S(1)} %get-tuple-element.34, f32[4,416,512,4]{2,1,3,0:T(8,128)} %get-tuple-element.39, pred[512,416]{0,1:T(8,128)(4,1)S(1)} %get-tuple-element.36, ...), kind=kOutput, calls=%fused_computation.5 | convolution fusion | flops 892862464 | bytes 23248896 | tf_op jit(solution)/shard_map/pkgd,rkd->kgpr/dot_general | solution.py:54
  311.6 4.4 %multiply_convert_fusion = bf16[4,128,4,512]{3,1,2,0:T(8,128)(2,1)S(1)} fusion(f32[4,128,4,512]{3,1,2,0:T(8,128)S(1)} %fusion.86, bf16[4,4,512,416]{2,3,1,0:T(8,128)(2,1)} %copy-done.9, bf16[416,4,128,1]{2,1,0,3:T(4,128)(2,1)S(1)} %bitcast.269), kind=kOutput, calls=%fused_computation.36 | convolution fusion | flops 875560960 | bytes 13533184 | tf_op jit(solution)/shard_map/kgpr,rkd->pkgd/dot_general | solution.py:60
  331.6 17.5 %all-to-all-done.4 = bf16[4,416,512]{2,1,0:T(8,128)(2,1)S(1)} async-done(((bf16[4,416,512]{2,1,0:T(8,128)(2,1)}), bf16[4,416,512]{2,1,0:T(8,128)(2,1)S(1)}, u32[]{:S(2)}, u32[]{:S(2)}) %all-to-all-start.4) | async-done | bytes 1703968 | tf_op jit(solution)/shard_map/all_to_all | solution.py:258
  357.9 16.7 %all-to-all-done.7 = bf16[4,416,512]{2,0,1:T(4,128)(2,1)S(1)} async-done(((bf16[4,416,512]{2,0,1:T(4,128)(2,1)}), bf16[4,416,512]{2,0,1:T(4,128)(2,1)S(1)}, u32[]{:S(2)}, u32[]{:S(2)}) %all-to-all-start.7) | async-done | bytes 1703968 | tf_op jit(solution)/shard_map/all_to_all | solution.py:264
  381.9 5.2 %copy.357 = bf16[4,2,208,512]{3,1,0,2:T(2,128)(2,1)} copy(bf16[4,2,208,512]{3,0,2,1:T(4,128)(2,1)} %bitcast.254) | data formatting | bytes 3407872 | tf_op jit(solution)/shard_map/all_to_all | solution.py:264
  387.1 5.7 %all_to_all.83 = bf16[4,208,1024]{2,0,1:T(4,128)(2,1)} reshape(bf16[4,208,2,512]{3,2,0,1:T(2,128)(2,1)} %bitcast.256) | data formatting | bytes 3407872 | tf_op jit(solution)/shard_map/all_to_all | solution.py:264
  402.3 5.1 %all_to_all.78 = bf16[4,208,1024]{2,1,0:T(8,128)(2,1)} reshape(bf16[4,208,2,512]{3,2,1,0:T(2,128)(2,1)} %bitcast.257) | data formatting | bytes 3407872 | tf_op jit(solution)/shard_map/all_to_all | solution.py:257
  (188 shorter events, 161.9 us)
Async XLA Ops:
  7.2 18.6 %copy-start = (bf16[2,208,1024]{2,1,0:T(8,128)(2,1)S(1)}, bf16[2,208,1024]{2,1,0:T(8,128)(2,1)}, u32[]{:S(2)}) copy-start(bf16[2,208,1024]{2,1,0:T(8,128)(2,1)} %param.12) | copy-start | bytes 2555908
  9.8 5.2 %copy-start.16 = (bf16[2,208,1024]{2,1,0:T(8,128)(2,1)S(1)}, bf16[2,208,1024]{2,1,0:T(8,128)(2,1)}, u32[]{:S(2)}) copy-start(bf16[2,208,1024]{2,1,0:T(8,128)(2,1)} %param.11) | copy-start | bytes 2555908
  16.8 6.2 %copy-start.26 = (bf16[1,128,2048]{2,1,0:T(8,128)(2,1)S(1)}, bf16[1,128,2048]{2,1,0:T(8,128)(2,1)}, u32[]{:S(2)}) copy-start(bf16[1,128,2048]{2,1,0:T(8,128)(2,1)} %param.10) | copy-start | bytes 1572868
  18.6 26.6 %all-to-all-start.2 = ((bf16[4,208,1024]{2,1,0:T(8,128)(2,1)}), bf16[4,208,1024]{2,1,0:T(8,128)(2,1)}, u32[]{:S(2)}, u32[]{:S(2)}) async-start(bf16[4,208,1024]{2,1,0:T(8,128)(2,1)} %copy.195), calls=%async_computation.2 | async-start | bytes 3407872 | tf_op jit(solution)/shard_map/all_to_all | solution.py:182
  23.0 117.4 %all-gather.3.cloned.1.call-start = ((), (), s32[]{:S(2)}) async-start(), calls=%async_computation.9 | async-start | bytes 2621440 | tf_op jit(solution)/shard_map/all_gather | solution.py:213
  45.1 25.0 %all-to-all-start = ((bf16[4,208,1024]{2,1,0:T(8,128)(2,1)}), bf16[4,208,1024]{2,1,0:T(8,128)(2,1)S(1)}, u32[]{:S(2)}, u32[]{:S(2)}) async-start(bf16[4,208,1024]{2,1,0:T(8,128)(2,1)} %copy.189), calls=%async_computation | async-start | bytes 3407872 | tf_op jit(solution)/shard_map/all_to_all | solution.py:189
  48.7 27.1 %copy-start.27 = (bf16[1,128,2048]{2,1,0:T(8,128)(2,1)S(1)}, bf16[1,128,2048]{2,1,0:T(8,128)(2,1)}, u32[]{:S(2)}) copy-start(bf16[1,128,2048]{2,1,0:T(8,128)(2,1)} %param.19) | copy-start | bytes 1572868
  53.0 24.2 %copy-start.41 = (s32[4]{0:T(128)S(1)}, s32[4]{0:T(128)}, u32[]{:S(2)}) copy-start(s32[4]{0:T(128)} %param.16) | copy-start | bytes 52
  71.4 29.2 %all-to-all-start.3 = ((bf16[4,208,1024]{1,0,2:T(4,128)(2,1)}), bf16[4,208,1024]{1,0,2:T(4,128)(2,1)S(1)}, u32[]{:S(2)}, u32[]{:S(2)}) async-start(bf16[4,208,1024]{1,0,2:T(4,128)(2,1)} %copy.196), calls=%async_computation.3 | async-start | bytes 4194304 | tf_op jit(solution)/shard_map/all_to_all | solution.py:181
  75.1 128.2 %all-gather.5.cloned.1.call-start = ((), (), s32[]{:S(2)}) async-start(), calls=%async_computation.11 | async-start | bytes 2621440 | tf_op jit(solution)/shard_map/all_gather | solution.py:214
  100.6 29.3 %all-to-all-start.1 = ((bf16[4,208,1024]{1,0,2:T(4,128)(2,1)}), bf16[4,208,1024]{1,0,2:T(4,128)(2,1)}, u32[]{:S(2)}, u32[]{:S(2)}) async-start(bf16[4,208,1024]{1,0,2:T(4,128)(2,1)} %copy.190), calls=%async_computation.1 | async-start | bytes 4194304 | tf_op jit(solution)/shard_map/all_to_all | solution.py:188
  105.4 165.5 %all-reduce.2.cloned.1.call-start = ((), (), s32[]{:S(2)}) async-start(), calls=%async_computation.10 | async-start | bytes 4194304 | tf_op jit(solution)/shard_map/psum | solution.py:221
  140.4 8.4 %copy-start.22 = (bf16[416,4,128]{2,1,0:T(4,128)(2,1)S(1)}, bf16[416,4,128]{2,1,0:T(4,128)(2,1)}, u32[]{:S(2)}) copy-start(bf16[416,4,128]{2,1,0:T(4,128)(2,1)} %reshape_squeeze.17) | copy-start | bytes 1277956
  140.4 8.4 %copy-start.38 = (bf16[512,4,4,128]{3,0,2,1:T(8,128)(2,1)S(1)}, bf16[512,4,4,128]{3,0,2,1:T(8,128)(2,1)}, u32[]{:S(2)}) copy-start(bf16[512,4,4,128]{3,0,2,1:T(8,128)(2,1)} %all-gather.3.cloned.1.call-done) | copy-start | bytes 6291460
  175.0 8.8 %copy-start.2 = (f32[4,416,512,4]{2,1,3,0:T(8,128)S(1)}, f32[4,416,512,4]{2,1,3,0:T(8,128)}, u32[]{:S(2)}) copy-start(f32[4,416,512,4]{2,1,3,0:T(8,128)} %get-tuple-element.39) | copy-start | bytes 40894468
  215.2 8.3 %copy-start.17 = (bf16[4,128,4,4,128]{4,1,3,2,0:T(8,128)(2,1)S(1)}, bf16[4,128,4,4,128]{4,1,3,2,0:T(8,128)(2,1)}, u32[]{:S(2)}) copy-start(bf16[4,128,4,4,128]{4,1,3,2,0:T(8,128)(2,1)} %copy.227) | copy-start | bytes 6291460
  236.5 34.4 %copy-start.8 = (bf16[512,4,4,128]{0,3,2,1:T(8,128)(2,1)S(1)}, bf16[512,4,4,128]{0,3,2,1:T(8,128)(2,1)}, u32[]{:S(2)}) copy-start(bf16[512,4,4,128]{0,3,2,1:T(8,128)(2,1)} %all-gather.5.cloned.1.call-done) | copy-start | bytes 6291460
  238.0 86.1 %all-to-all-start.6 = ((bf16[4,416,512]{2,1,0:T(8,128)(2,1)}), bf16[4,416,512]{2,1,0:T(8,128)(2,1)}, u32[]{:S(2)}, u32[]{:S(2)}) async-start(bf16[4,416,512]{2,1,0:T(8,128)(2,1)} %copy.235), calls=%async_computation.6 | async-start | bytes 3407872 | tf_op jit(solution)/shard_map/all_to_all | solution.py:265
  242.4 174.0 %reduce-scatter.4.cloned.1.call-start = ((), (), s32[]{:S(2)}) async-start(), calls=%async_computation.12 | async-start | bytes 2621440
  275.4 10.2 %copy-start.39 = (bf16[512,4,4,128]{3,0,2,1:T(8,128)(2,1)S(1)}, bf16[512,4,4,128]{3,0,2,1:T(8,128)(2,1)}, u32[]{:S(2)}) copy-start(bf16[512,4,4,128]{3,0,2,1:T(8,128)(2,1)} %all-gather.3.cloned.1.call-done) | copy-start | bytes 6291460
  293.5 10.2 %copy-start.40 = (bf16[512,4,4,128]{3,0,2,1:T(8,128)(2,1)S(1)}, bf16[512,4,4,128]{3,0,2,1:T(8,128)(2,1)}, u32[]{:S(2)}) copy-start(bf16[512,4,4,128]{3,0,2,1:T(8,128)(2,1)} %all-gather.3.cloned.1.call-done) | copy-start | bytes 6291460
  324.0 25.0 %all-to-all-start.4 = ((bf16[4,416,512]{2,1,0:T(8,128)(2,1)}), bf16[4,416,512]{2,1,0:T(8,128)(2,1)S(1)}, u32[]{:S(2)}, u32[]{:S(2)}) async-start(bf16[4,416,512]{2,1,0:T(8,128)(2,1)} %copy.219), calls=%async_computation.4 | async-start | bytes 3407872 | tf_op jit(solution)/shard_map/all_to_all | solution.py:258
  350.2 24.4 %all-to-all-start.7 = ((bf16[4,416,512]{2,0,1:T(4,128)(2,1)}), bf16[4,416,512]{2,0,1:T(4,128)(2,1)S(1)}, u32[]{:S(2)}, u32[]{:S(2)}) async-start(bf16[4,416,512]{2,0,1:T(4,128)(2,1)} %copy.236), calls=%async_computation.7 | async-start | bytes 3407872 | tf_op jit(solution)/shard_map/all_to_all | solution.py:264
  375.8 23.5 %all-to-all-start.5 = ((bf16[4,416,512]{2,0,1:T(4,128)(2,1)}), bf16[4,416,512]{2,0,1:T(4,128)(2,1)S(1)}, u32[]{:S(2)}, u32[]{:S(2)}) async-start(bf16[4,416,512]{2,0,1:T(4,128)(2,1)} %copy.220), calls=%async_computation.5 | async-start | bytes 3407872 | tf_op jit(solution)/shard_map/all_to_all | solution.py:257
  (30 other events, 81.7 us)
Sparse Core Ops, SparseCore 0:
  25.9 48.7 all-gather.2
  78.1 47.8 all-gather.4
  187.8 82.9 all-reduce.1
  318.7 42.6 reduce-scatter.3
where the time goes:
time: 434 us; the launch traced here: 427 us
  waiting for transfers between devices  128 us (29%)
  local copies, waits for them, and re-layouts  109 us (25%)
  matrix products  85 us (20%)
  other arithmetic  36.4 us (8%)
  starting transfers between devices  32.3 us (7%)
  blocking collectives  19.6 us (5%)
  between operations  15.7 us (4%)
    psum x1, waiting for transfers between devices, shards(): lax.psum(part_weighted.astype(jnp.bfloat16), 'seq').astype(jnp.float32)  28.4 us
    unnamed x92, local copies, waits for them, and re-layouts  26.6 us
    psum x1, blocking collectives, shards(): lax.psum(part_sum.astype(jnp.bfloat16), 'seq').astype(jnp.float32)  19.6 us
    all_to_all x1, waiting for transfers between devices, shards(): lax.all_to_all(back_keys, 'conv', split_axis=0, concat_axis=0, tiled=True)  17.5 us
    all_to_all x1, waiting for transfers between devices, shards(): lax.all_to_all(lax.all_to_all(outgoing_keys, 'conv', split_axis=0, concat...  17.2 us
    all_to_all x1, waiting for transfers between devices, shards(): lax.all_to_all(send_values, 'conv', split_axis=0, concat_axis=0, tiled=True)  17.2 us
    all_to_all x1, waiting for transfers between devices, shards(): lax.all_to_all(lax.all_to_all(back_values, 'conv', split_axis=0, concat_a...  16.7 us
    all_to_all x1, waiting for transfers between devices, shards(): lax.all_to_all(outgoing_keys, 'conv', split_axis=0, concat_axis=0, tiled=...  16.1 us
  transfers between devices with their start and end apart: 12, of which 8 were waited for; matrix products, arithmetic and copies ran while one was open for 45% of the time, Pallas kernels for 0%

commit v1 on v0

--- a/solution.py
+++ b/solution.py
@@ -4,6 +4,7 @@
 import jax.numpy as jnp
 from jax import lax
 from jax.sharding import PartitionSpec as P
+from jax.lax import all_gather
 
 TILE = 1601
 EPSILON = 1e-05
@@ -218,7 +219,9 @@
         all_queries, tile_keys, tile_values, seen_all, row_start, score_scale
     )
     all_weighted, all_weight_sum = (
-        lax.psum(part_weighted.astype(jnp.bfloat16), "seq").astype(jnp.float32),
+        jnp.sum(all_gather(part_weighted.astype(jnp.bfloat16), axis_name="seq"), axis=0).astype(
+            jnp.float32
+        ),
         lax.psum(part_sum.astype(jnp.bfloat16), "seq").astype(jnp.float32),
     )
     safe_all = jnp.where(all_weight_sum > 0, all_weight_sum, 1.0)

time: 434 us -> 512 us (1.18)
  waiting for transfers between devices: 128 us -> 179 us
  other arithmetic: 36.4 us -> 49.4 us
  local copies, waits for them, and re-layouts: 109 us -> 120 us
    all_gather x0 -> x1, waiting for transfers between devices: none -> 80 us  [shards(): all_gather(part_weighted.astype(jnp.bfloat16), axis_name='seq')]
    psum x1 -> x0, waiting for transfers between devices: 28.4 us -> none  [shards(): lax.psum(part_weighted.astype(jnp.bfloat16), 'seq').astype(jnp.float32)]
    all_gather x0 -> x1, local copies, waits for them, and re-layouts: none -> 14.6 us  [shards(): all_gather(part_weighted.astype(jnp.bfloat16), axis_name='seq')]
    reduce_sum x0 -> x1, other arithmetic: none -> 13 us  [shards(): jnp.sum(all_gather(part_weighted.astype(jnp.bfloat16), axis_name='seq'),...]
    reshape x2 -> x0, local copies, waits for them, and re-layouts: 5.14 us -> none  [tile_gradients(): grad_bf.reshape(block_count, block_tokens, kv_local, group_size, head_size)]
    unnamed x92 -> x101, local copies, waits for them, and re-layouts: 26.6 us -> 24.6 us
  transfers between devices with their start and end apart: 12 -> 12, of which waited for: 8 -> 8; matrix products, arithmetic and copies ran while one was open for 45% -> 44% of each run, Pallas kernels for 0% -> 0%
where the time goes in v1:
time: 512 us; the launch traced here: 504 us
  waiting for transfers between devices  179 us (35%)
  local copies, waits for them, and re-layouts  120 us (23%)
  matrix products  86.8 us (17%)
  other arithmetic  49.4 us (10%)
  starting transfers between devices  32.3 us (6%)
  blocking collectives  20.3 us (4%)
  between operations  15.8 us (3%)
    all_gather x1, waiting for transfers between devices, shards(): all_gather(part_weighted.astype(jnp.bfloat16), axis_name='seq')  80 us
    unnamed x101, local copies, waits for them, and re-layouts  24.6 us
    psum x1, blocking collectives, shards(): lax.psum(part_sum.astype(jnp.bfloat16), 'seq').astype(jnp.float32)  20.3 us
    all_to_all x1, waiting for transfers between devices, shards(): lax.all_to_all(back_keys, 'conv', split_axis=0, concat_axis=0, tiled=True)  17.5 us
    all_to_all x1, waiting for transfers between devices, shards(): lax.all_to_all(send_values, 'conv', split_axis=0, concat_axis=0, tiled=True)  17.2 us
    all_to_all x1, waiting for transfers between devices, shards(): lax.all_to_all(lax.all_to_all(outgoing_keys, 'conv', split_axis=0, concat...  17 us
    all_to_all x1, waiting for transfers between devices, shards(): lax.all_to_all(lax.all_to_all(back_values, 'conv', split_axis=0, concat_a...  16.7 us
    all_to_all x1, waiting for transfers between devices, shards(): lax.all_to_all(outgoing_keys, 'conv', split_axis=0, concat_axis=0, tiled=...  16.2 us
  transfers between devices with their start and end apart: 12, of which 8 were waited for; matrix products, arithmetic and copies ran while one was open for 44% of the time, Pallas kernels for 0%

profile of v1, /device:TPU:0, one launch (start us, length us, event | category | flops | bytes accessed | tf_op | source)
XLA Modules:
  0.0 503.9 jit_solution(2944736521895584661)
XLA Ops:
  29.0 16.2 %all-to-all-done.2 = bf16[4,208,1024]{2,1,0:T(8,128)(2,1)} async-done(((bf16[4,208,1024]{2,1,0:T(8,128)(2,1)}), bf16[4,208,1024]{2,1,0:T(8,128)(2,1)}, u32[]{:S(2)}, u32[]{:S(2)}) %all-to-all-start.2) | async-done | bytes 1703968 | tf_op jit(solution)/shard_map/all_to_all | solution.py:183
  53.0 17.2 %all-to-all-done = bf16[4,208,1024]{2,1,0:T(8,128)(2,1)S(1)} async-done(((bf16[4,208,1024]{2,1,0:T(8,128)(2,1)}), bf16[4,208,1024]{2,1,0:T(8,128)(2,1)S(1)}, u32[]{:S(2)}, u32[]{:S(2)}) %all-to-all-start) | async-done | bytes 1703968 | tf_op jit(solution)/shard_map/all_to_all | solution.py:190
  83.6 17.0 %all-to-all-done.3 = bf16[4,208,1024]{1,0,2:T(4,128)(2,1)S(1)} async-done(((bf16[4,208,1024]{1,0,2:T(4,128)(2,1)}), bf16[4,208,1024]{1,0,2:T(4,128)(2,1)S(1)}, u32[]{:S(2)}, u32[]{:S(2)}) %all-to-all-start.3) | async-done | bytes 1703968 | tf_op jit(solution)/shard_map/all_to_all | solution.py:182
  100.6 4.8 all-to-all-start.1
  117.9 12.0 %all-to-all-done.1 = bf16[4,208,1024]{1,0,2:T(4,128)(2,1)} async-done(((bf16[4,208,1024]{1,0,2:T(4,128)(2,1)}), bf16[4,208,1024]{1,0,2:T(4,128)(2,1)}, u32[]{:S(2)}, u32[]{:S(2)}) %all-to-all-start.1) | async-done | bytes 1703968 | tf_op jit(solution)/shard_map/all_to_all | solution.py:189
  130.0 5.4 %copy.189 = bf16[4,208,2,512]{3,0,1,2:T(4,128)(2,1)S(1)} copy(bf16[4,208,2,512]{1,0,3,2:T(4,128)(2,1)} %bitcast.2) | data formatting | bytes 3407872 | tf_op jit(solution)/shard_map/all_to_all | solution.py:189
  140.4 8.7 %fusion.8 = (f32[4,4,512]{2,1,0:T(4,128)S(1)}, f32[4,416,512,4]{2,1,3,0:T(8,128)}) fusion(pred[512,416]{0,1:T(8,128)(4,1)S(1)} %get-tuple-element.37, bf16[512,4,4,128]{3,0,2,1:T(8,128)(2,1)} %all-gather.5.cloned.1.call-done, bf16[416,4,128,1]{2,1,0,3:T(4,128)(2,1)S(1)} %bitcast.269), kind=kOutput, calls=%fused_computation.12 | convolution fusion | flops 882630656 | bytes 16400384 | tf_op jit(solution)/shard_map/pkgd,rkd->kgpr/dot_general | solution.py:25
  152.6 11.1 %fusion.10 = f32[4,128,4,512]{3,1,2,0:T(8,128)S(1)} fusion(f32[4,416,512,4]{2,1,3,0:T(8,128)} %get-tuple-element.41, pred[512,416]{0,1:T(8,128)(4,1)S(1)} %get-tuple-element.37, bf16[416,4,128,1]{2,1,0,3:T(4,128)(2,1)S(1)} %bitcast.261), kind=kOutput, calls=%fused_computation.14 | convolution fusion | flops 882638848 | bytes 18464768 | tf_op jit(solution)/shard_map/kgpr,rkd->pkgd/dot_general | solution.py:33
  167.7 20.3 %psum.7 = bf16[4,4,512]{2,1,0:T(4,128)(2,1)S(1)} all-reduce(bf16[4,4,512]{2,1,0:T(4,128)(2,1)S(1)} %add_convert_fusion.1), channel_id=1, replica_groups=mesh['conv'=4,'seq'=4,'tensor'=2] {'seq'}, use_global_device_ids=true, to_apply=%region_5.6 | all-reduce | flops 8192 | bytes 32768 | tf_op jit(solution)/shard_map/psum | solution.py:225
  188.0 15.4 %convert_bitcast_fusion.1 = (bf16[4,4,52,4,8,128]{5,4,3,2,1,0:T(8,128)(2,1)}, bf16[4,4,52,4,8,128]{5,4,3,2,1,0:T(8,128)(2,1)}) fusion(f32[4,4,512]{2,1,0:T(4,128)S(1)} %get-tuple-element.34, f32[4,416,512,4]{2,1,3,0:T(8,128)} %copy-done.2, pred[512,416]{0,1:T(8,128)(4,1)S(1)} %get-tuple-element.36, f32[4,416,512,4]{2,1,3,0:T(8,128)} %get-tuple-element.41, ...), kind=kLoop, calls=%fused_computation.29 | loop fusion | flops 27262976 | bytes 41353216
  203.4 6.8 %fusion.64 = bf16[4,416,4,128]{3,1,2,0:T(8,128)(2,1)} fusion(bf16[4,128,4,4,128]{4,1,0,3,2:T(8,128)(2,1)} %bitcast.265, bf16[4,4,52,4,8,128]{5,4,3,2,1,0:T(8,128)(2,1)} %get-tuple-element.32), kind=kOutput, calls=%fused_computation.71 | convolution fusion | flops 873267200 | bytes 10616832 | tf_op jit(solution)/shard_map/kgbpr,bpkgd->brkd/dot_general | solution.py:77
  218.4 6.1 %fusion.69 = bf16[4,416,4,128]{3,1,2,0:T(8,128)(2,1)} fusion(bf16[4,128,4,4,128]{4,1,0,3,2:T(8,128)(2,1)S(1)} %bitcast.266, bf16[4,4,52,4,8,128]{5,4,3,2,1,0:T(8,128)(2,1)} %get-tuple-element.33), kind=kOutput, calls=%fused_computation.72 | convolution fusion | flops 873267200 | bytes 10616832 | tf_op jit(solution)/shard_map/kgbpr,bpkgd->brkd/dot_general | solution.py:77
  237.4 80.0 %all-gather.9.cloned.1.call-done = bf16[2048,4,4,128]{0,3,2,1:T(8,128)(2,1)} async-done(((bf16[512,4,4,128]{0,3,2,1:T(8,128)(2,1)}), bf16[2048,4,4,128]{0,3,2,1:T(8,128)(2,1)}) %all-gather.9.cloned.1.call-update) | async-done | bytes 8388624 | tf_op jit(solution)/shard_map/all_gather | solution.py:222
  317.4 14.6 %reshape.250 = bf16[4,512,4,4,128]{1,0,4,3,2:T(4,128)(2,1)} reshape(bf16[2048,4,4,128]{0,3,2,1:T(8,128)(2,1)} %all-gather.9.cloned.1.call-done) | data formatting | bytes 16777216 | tf_op jit(solution)/shard_map/all_gather | solution.py:222
  332.1 13.0 %reduce_sum.121 = bf16[512,4,4,128]{0,3,2,1:T(8,128)(2,1)} reduce(bf16[4,512,4,4,128]{1,0,4,3,2:T(4,128)(2,1)} %reshape.250, bf16[]{:T(256)} %constant.30.clone.1), dimensions={0}, to_apply=%region_2.3 | reduce | flops 3145728 | bytes 10485762 | tf_op jit(solution)/shard_map/reduce_sum | solution.py:222
  348.1 4.5 multiply_reduce_fusion
  352.6 7.4 %fusion.1 = bf16[4,4,512,416]{2,3,1,0:T(8,128)(2,1)S(1)} fusion(bf16[512,4,4,128]{3,0,2,1:T(8,128)(2,1)S(1)} %copy-done.17, f32[4,4,512]{2,1,0:T(4,128)S(1)} %bitcast.274, f32[4,4,512]{2,1,0:T(4,128)S(1)} %get-tuple-element.34, f32[4,416,512,4]{2,1,3,0:T(8,128)} %get-tuple-element.41, pred[512,416]{0,1:T(8,128)(4,1)S(1)} %get-tuple-element.37, ...), kind=kOutput, calls=%fused_computation.2 | convolution fusion | flops 892862464 | bytes 23248896 | tf_op jit(solution)/shard_map/pkgd,rkd->kgpr/dot_general | solution.py:55
  370.8 7.5 %fusion.3 = bf16[4,4,512,416]{2,3,1,0:T(8,128)(2,1)S(1)} fusion(bf16[512,4,4,128]{3,0,2,1:T(8,128)(2,1)S(1)} %copy-done.18, f32[4,4,512]{2,1,0:T(4,128)S(1)} %bitcast.275, f32[4,4,512]{2,1,0:T(4,128)S(1)} %get-tuple-element.34, f32[4,416,512,4]{2,1,3,0:T(8,128)} %copy-done.2, pred[512,416]{0,1:T(8,128)(4,1)S(1)} %get-tuple-element.36, ...), kind=kOutput, calls=%fused_computation.5 | convolution fusion | flops 892862464 | bytes 23248896 | tf_op jit(solution)/shard_map/pkgd,rkd->kgpr/dot_general | solution.py:55
  389.1 4.4 multiply_convert_fusion
  408.9 17.5 %all-to-all-done.4 = bf16[4,416,512]{2,1,0:T(8,128)(2,1)S(1)} async-done(((bf16[4,416,512]{2,1,0:T(8,128)(2,1)}), bf16[4,416,512]{2,1,0:T(8,128)(2,1)S(1)}, u32[]{:S(2)}, u32[]{:S(2)}) %all-to-all-start.4) | async-done | bytes 1703968 | tf_op jit(solution)/shard_map/all_to_all | solution.py:261
  435.3 16.7 %all-to-all-done.7 = bf16[4,416,512]{2,0,1:T(4,128)(2,1)S(1)} async-done(((bf16[4,416,512]{2,0,1:T(4,128)(2,1)}), bf16[4,416,512]{2,0,1:T(4,128)(2,1)S(1)}, u32[]{:S(2)}, u32[]{:S(2)}) %all-to-all-start.7) | async-done | bytes 1703968 | tf_op jit(solution)/shard_map/all_to_all | solution.py:267
  456.9 5.3 %copy.362 = bf16[4,2,208,512]{3,1,0,2:T(2,128)(2,1)} copy(bf16[4,2,208,512]{3,0,2,1:T(4,128)(2,1)} %bitcast.253) | data formatting | bytes 3407872 | tf_op jit(solution)/shard_map/all_to_all | solution.py:267
  462.1 5.7 %all_to_all.83 = bf16[4,208,1024]{2,0,1:T(4,128)(2,1)} reshape(bf16[4,208,2,512]{3,2,0,1:T(2,128)(2,1)} %bitcast.255) | data formatting | bytes 3407872 | tf_op jit(solution)/shard_map/all_to_all | solution.py:267
  479.6 5.1 %all_to_all.78 = bf16[4,208,1024]{2,1,0:T(8,128)(2,1)} reshape(bf16[4,208,2,512]{3,2,1,0:T(2,128)(2,1)} %bitcast.256) | data formatting | bytes 3407872 | tf_op jit(solution)/shard_map/all_to_all | solution.py:260
  (199 shorter events, 165.5 us)
Async XLA Ops:
  7.2 18.6 %copy-start = (bf16[2,208,1024]{2,1,0:T(8,128)(2,1)S(1)}, bf16[2,208,1024]{2,1,0:T(8,128)(2,1)}, u32[]{:S(2)}) copy-start(bf16[2,208,1024]{2,1,0:T(8,128)(2,1)} %param.12) | copy-start | bytes 2555908
  15.1 10.7 %copy-start.40 = (pred[4,2]{0,1:T(4,128)(4,1)}, pred[4,2]{0,1:T(4,128)(4,1)S(1)}, u32[]{:S(2)}) copy-start(pred[4,2]{0,1:T(4,128)(4,1)S(1)} %broadcast_compare_fusion) | copy-start | bytes 28
  18.6 26.6 %all-to-all-start.2 = ((bf16[4,208,1024]{2,1,0:T(8,128)(2,1)}), bf16[4,208,1024]{2,1,0:T(8,128)(2,1)}, u32[]{:S(2)}, u32[]{:S(2)}) async-start(bf16[4,208,1024]{2,1,0:T(8,128)(2,1)} %copy.193), calls=%async_computation.2 | async-start | bytes 3407872 | tf_op jit(solution)/shard_map/all_to_all | solution.py:183
  23.0 117.4 %all-gather.5.cloned.1.call-start = ((), (), s32[]{:S(2)}) async-start(), calls=%async_computation.9 | async-start | bytes 2621440 | tf_op jit(solution)/shard_map/all_gather | solution.py:214
  45.2 25.0 %all-to-all-start = ((bf16[4,208,1024]{2,1,0:T(8,128)(2,1)}), bf16[4,208,1024]{2,1,0:T(8,128)(2,1)S(1)}, u32[]{:S(2)}, u32[]{:S(2)}) async-start(bf16[4,208,1024]{2,1,0:T(8,128)(2,1)} %copy.187), calls=%async_computation | async-start | bytes 3407872 | tf_op jit(solution)/shard_map/all_to_all | solution.py:190
  48.7 27.1 %copy-start.28 = (bf16[1,128,2048]{2,1,0:T(8,128)(2,1)S(1)}, bf16[1,128,2048]{2,1,0:T(8,128)(2,1)}, u32[]{:S(2)}) copy-start(bf16[1,128,2048]{2,1,0:T(8,128)(2,1)} %param.19) | copy-start | bytes 1572868
  53.0 24.5 %copy-start.45 = (s32[4]{0:T(128)S(1)}, s32[4]{0:T(128)}, u32[]{:S(2)}) copy-start(s32[4]{0:T(128)} %param.16) | copy-start | bytes 52
  71.4 29.2 %all-to-all-start.3 = ((bf16[4,208,1024]{1,0,2:T(4,128)(2,1)}), bf16[4,208,1024]{1,0,2:T(4,128)(2,1)S(1)}, u32[]{:S(2)}, u32[]{:S(2)}) async-start(bf16[4,208,1024]{1,0,2:T(4,128)(2,1)} %copy.194), calls=%async_computation.3 | async-start | bytes 4194304 | tf_op jit(solution)/shard_map/all_to_all | solution.py:182
  75.2 128.2 %all-gather.7.cloned.1.call-start = ((), (), s32[]{:S(2)}) async-start(), calls=%async_computation.10 | async-start | bytes 2621440 | tf_op jit(solution)/shard_map/all_gather | solution.py:215
  100.6 29.4 %all-to-all-start.1 = ((bf16[4,208,1024]{1,0,2:T(4,128)(2,1)}), bf16[4,208,1024]{1,0,2:T(4,128)(2,1)}, u32[]{:S(2)}, u32[]{:S(2)}) async-start(bf16[4,208,1024]{1,0,2:T(4,128)(2,1)} %copy.188), calls=%async_computation.1 | async-start | bytes 4194304 | tf_op jit(solution)/shard_map/all_to_all | solution.py:189
  105.4 212.0 %all-gather.9.cloned.1.call-start = ((), (), s32[]{:S(2)}) async-start(), calls=%async_computation.11 | async-start | bytes 10485760 | tf_op jit(solution)/shard_map/all_gather | solution.py:222
  140.4 8.7 %copy-start.23 = (bf16[416,4,128]{2,1,0:T(4,128)(2,1)S(1)}, bf16[416,4,128]{2,1,0:T(4,128)(2,1)}, u32[]{:S(2)}) copy-start(bf16[416,4,128]{2,1,0:T(4,128)(2,1)} %reshape_squeeze.17) | copy-start | bytes 1277956
  140.4 8.7 %copy-start.42 = (bf16[512,4,4,128]{3,0,2,1:T(8,128)(2,1)S(1)}, bf16[512,4,4,128]{3,0,2,1:T(8,128)(2,1)}, u32[]{:S(2)}) copy-start(bf16[512,4,4,128]{3,0,2,1:T(8,128)(2,1)} %all-gather.5.cloned.1.call-done) | copy-start | bytes 6291460
  152.6 11.2 %copy-start.2 = (f32[4,416,512,4]{2,1,3,0:T(8,128)}, f32[4,416,512,4]{2,1,3,0:T(8,128)S(1)}, u32[]{:S(2)}) copy-start(f32[4,416,512,4]{2,1,3,0:T(8,128)S(1)} %get-tuple-element.39) | copy-start | bytes 40894468
  210.1 8.3 %copy-start.16 = (bf16[512,4,4,128]{3,0,2,1:T(8,128)(2,1)S(1)}, bf16[512,4,4,128]{3,0,2,1:T(8,128)(2,1)}, u32[]{:S(2)}) copy-start(bf16[512,4,4,128]{3,0,2,1:T(8,128)(2,1)} %all-gather.7.cloned.1.call-done) | copy-start | bytes 6291460
  233.0 168.4 %all-to-all-start.6 = ((bf16[4,416,512]{2,1,0:T(8,128)(2,1)}), bf16[4,416,512]{2,1,0:T(8,128)(2,1)}, u32[]{:S(2)}, u32[]{:S(2)}) async-start(bf16[4,416,512]{2,1,0:T(8,128)(2,1)} %copy.234), calls=%async_computation.6 | async-start | bytes 3407872 | tf_op jit(solution)/shard_map/all_to_all | solution.py:268
  237.4 256.4 %reduce-scatter.4.cloned.1.call-start = ((), (), s32[]{:S(2)}) async-start(), calls=%async_computation.12 | async-start | bytes 2621440
  352.6 10.1 %copy-start.43 = (bf16[512,4,4,128]{3,0,2,1:T(8,128)(2,1)S(1)}, bf16[512,4,4,128]{3,0,2,1:T(8,128)(2,1)}, u32[]{:S(2)}) copy-start(bf16[512,4,4,128]{3,0,2,1:T(8,128)(2,1)} %all-gather.5.cloned.1.call-done) | copy-start | bytes 6291460
  370.8 10.4 %copy-start.44 = (bf16[512,4,4,128]{3,0,2,1:T(8,128)(2,1)S(1)}, bf16[512,4,4,128]{3,0,2,1:T(8,128)(2,1)}, u32[]{:S(2)}) copy-start(bf16[512,4,4,128]{3,0,2,1:T(8,128)(2,1)} %all-gather.5.cloned.1.call-done) | copy-start | bytes 6291460
  401.4 25.0 %all-to-all-start.4 = ((bf16[4,416,512]{2,1,0:T(8,128)(2,1)}), bf16[4,416,512]{2,1,0:T(8,128)(2,1)S(1)}, u32[]{:S(2)}, u32[]{:S(2)}) async-start(bf16[4,416,512]{2,1,0:T(8,128)(2,1)} %copy.218), calls=%async_computation.4 | async-start | bytes 3407872 | tf_op jit(solution)/shard_map/all_to_all | solution.py:261
  427.6 24.4 %all-to-all-start.7 = ((bf16[4,416,512]{2,0,1:T(4,128)(2,1)}), bf16[4,416,512]{2,0,1:T(4,128)(2,1)S(1)}, u32[]{:S(2)}, u32[]{:S(2)}) async-start(bf16[4,416,512]{2,0,1:T(4,128)(2,1)} %copy.235), calls=%async_computation.7 | async-start | bytes 3407872 | tf_op jit(solution)/shard_map/all_to_all | solution.py:267
  431.3 25.6 %copy-start.36 = (f32[128]{0:T(128)S(1)}, f32[128]{0:T(128)}, u32[]{:S(2)}) copy-start(f32[128]{0:T(128)} %param.13) | copy-start | bytes 1540
  453.1 23.5 %all-to-all-start.5 = ((bf16[4,416,512]{2,0,1:T(4,128)(2,1)}), bf16[4,416,512]{2,0,1:T(4,128)(2,1)S(1)}, u32[]{:S(2)}, u32[]{:S(2)}) async-start(bf16[4,416,512]{2,0,1:T(4,128)(2,1)} %copy.219), calls=%async_computation.5 | async-start | bytes 3407872 | tf_op jit(solution)/shard_map/all_to_all | solution.py:260
  456.9 10.9 %copy-start.41 = (pred[4,2]{0,1:T(4,128)(4,1)S(1)}, pred[4,2]{0,1:T(4,128)(4,1)}, u32[]{:S(2)}) copy-start(pred[4,2]{0,1:T(4,128)(4,1)} %copy-done.40) | copy-start | bytes 28
  (34 other events, 102.5 us)
Sparse Core Ops, SparseCore 0:
  25.9 48.8 all-gather.4
  78.1 47.2 all-gather.6
  167.8 149.5 all-gather.8
  396.2 41.8 reduce-scatter.3
